TPU v7x, 128 devices: a whole 4x4x4 slice. The times are simulated.
128 devices in a mesh: space: 32 (over x, y, core), tm: 2 (over z_hi), op: 2 (over z_lo).
Axes of the slice: x: 4, y: 4, z: 4 (z_hi: 2, z_lo: 2; z = z_hi * 2 + z_lo), core: 2. Of those that a mesh axis runs over, the one named last changes fastest.
Arguments:
- eigvecs: bfloat16 [2, 2, 256, 3, 64, 256], P('tm', None, None, None, 'space'), may hold values from -6 to 6
- links: float32 [2, 3, 3, 3, 2, 64, 256], P('tm', None, None, None, None, 'space'), may hold values from -2.5 to 2.5
- momenta: int32 [4, 3], P('op'), may hold values from -2 to 2
- coef_num: int32 [4, 4, 3], P(None, 'op'), may hold values from -3 to 3
- coef_den: int32 [4], replicated, may hold values from 1 to 6
- peram: bfloat16 [2, 256, 4, 4, 2, 256], P('tm'), may hold values from -0.25 to 0.25
Outputs:
- quark_lines: float32 [2, 4, 4, 4, 2, 256, 256], P('tm', 'op', None, None, None, 'space')
All inputs are finite; a program needn't handle non-finite values.
Results may differ from a plain program's by a relative error of at most 0.0053.
Values may be sent and summed in bfloat16 or wider, within the bound.
A program may use at most 128 MiB of HBM per device.

v0:
```python
import functools
import math

import jax
import jax.numpy as jnp
from jax import lax
from jax.experimental import pallas as pl
from jax.experimental.pallas import tpu as pltpu
from jax.sharding import PartitionSpec as P

MESH = pl.DeviceIdType.MESH
F32 = jnp.float32
BF16 = jnp.bfloat16
NS = 32
NX = 64
LY = 32
LZ = 8
PL = LY * LZ
NV = 256
NB = NV // 2
HEL = 4
SCALE = 1.0 / math.sqrt(3.0 * NX * LY * LZ)
WROW = 108


def nt_dot(a, b):
    return lax.dot_general(a, b, (((1,), (1,)), ((), ())), preferred_element_type=F32)


def kernel(mom, num, den, lk, v2, piece, out,
           xp, xm, halo_l, wloc, wrem, bc, vs, perm, shf, dbuf, pbuf, rbuf, tbuf, sbuf, obuf,
           s_halo, r_up, r_dn, r_lk, s_w, r_w, s_z, r_z, s_g, r_g1, r_g2, r_sib, s_rs, r_rs, s_o, r_o):
    me = lax.axis_index("space")
    tm = lax.axis_index("tm")
    op = lax.axis_index("op")

    def dev(space, t, o):
        return {"space": space, "tm": t, "op": o}

    def plane_dev(space):
        return dev(space, tm, op)

    def remote(src, dst, ssem, rsem, where):
        return pltpu.make_async_remote_copy(src_ref=src, dst_ref=dst, send_sem=ssem, recv_sem=rsem,
                                            device_id=where, device_id_type=MESH)

    core = lax.rem(me, 2)
    chip = me // 2
    cx = chip // 4
    cy = lax.rem(chip, 4)
    sib = me + 1 - 2 * core
    nxt = lax.rem(me + 1, NS)
    prv = lax.rem(me + NS - 1, NS)

    barrier = pltpu.get_barrier_semaphore()

    @pl.loop(1, NS)
    def _(d):
        pl.semaphore_signal(barrier, inc=1, device_id=plane_dev(lax.rem(me + d, NS)), device_id_type=MESH)

    pl.semaphore_signal(barrier, inc=1, device_id=dev(me, tm, 1 - op), device_id_type=MESH)
    pl.semaphore_signal(barrier, inc=1, device_id=dev(me, 1 - tm, 1 - op), device_id_type=MESH)
    pl.semaphore_wait(barrier, NS + 1)

    z_copy = remote(piece, tbuf.at[me], s_z, r_z, dev(me, 1 - tm, 1 - op))
    z_copy.start()

    brow = pl.multiple_of(op * NB, NB)
    halo = []
    for f in range(6):
        ri, c = f // 3, f % 3
        rows = pl.ds(pl.multiple_of(ri * NV + brow, NB), NB)
        up = remote(v2.at[rows, pl.ds(c * 2 * PL, PL)], xp.at[f, :, pl.ds(PL, PL)],
                    s_halo.at[f], r_up.at[f], plane_dev(prv))
        dn = remote(v2.at[rows, pl.ds(c * 2 * PL + PL, PL)], xm.at[f, :, pl.ds(0, PL)],
                    s_halo.at[6 + f], r_dn.at[f], plane_dev(nxt))
        up.start()
        dn.start()
        halo += [up, dn]
    lk_copy = remote(lk.at[pl.ds(0, 18)], halo_l, s_halo.at[12], r_lk, plane_dev(nxt))
    lk_copy.start()
    halo.append(lk_copy)

    site = lax.broadcasted_iota(jnp.int32, (8, PL), 1)
    yy = site // LZ
    zz = lax.rem(site, LZ)
    inv = [SCALE / (jnp.zeros((8, PL), F32) + den[h].astype(F32)) for h in range(HEL)]
    for plane in range(2):
        phase = []
        for p in range(2):
            turn = (mom[p, 0] * (2 * me + plane)) & (NX - 1)
            turn = turn + 2 * ((mom[p, 1] * yy) & (LY - 1)) + 8 * ((mom[p, 2] * zz) & (LZ - 1))
            theta = (2.0 * math.pi / NX) * turn.astype(F32)
            phase.append((jnp.cos(theta), -jnp.sin(theta)))
        for h in range(HEL):
            for j in range(3):
                n0 = num[h, 0, j].astype(F32)
                n1 = num[h, 1, j].astype(F32)
                for ri in range(2):
                    w = (phase[0][ri] * n0 + phase[1][ri] * n1) * inv[h]
                    row = (h * 3 + j) * 2 + ri
                    wloc[plane, row:row + 1, :] = w[0:1]
    w_copy = remote(wloc, wrem, s_w, r_w, dev(me, tm, 1 - op))
    w_copy.start()

    for f in range(6):
        ri, c = f // 3, f % 3
        rows = pl.ds(pl.multiple_of(ri * NV + brow, NB), NB)
        p0 = v2[rows, c * 2 * PL:c * 2 * PL + PL]
        p1 = v2[rows, c * 2 * PL + PL:(c + 1) * 2 * PL]
        xp[f, :, 0:PL] = p1
        xm[f, :, PL:2 * PL] = p0
        vs[0, f * NB:(f + 1) * NB, :] = p0
        vs[1, f * NB:(f + 1) * NB, :] = p1
    r_i = lax.broadcasted_iota(jnp.int32, (PL, PL), 0)
    c_i = lax.broadcasted_iota(jnp.int32, (PL, PL), 1)
    zc = c_i & (LZ - 1)
    sources = [(c_i + LZ) & (PL - 1), (c_i - LZ) & (PL - 1),
               c_i - zc + ((zc + 1) & (LZ - 1)), c_i - zc + ((zc - 1) & (LZ - 1))]
    for q in range(4):
        perm[q] = jnp.where(r_i == sources[q], 1.0, 0.0).astype(BF16)
    for q in range(4):
        for plane in range(2):
            @pl.loop(0, 3)
            def _(m):
                rows = pl.ds(pl.multiple_of(m * 256, 256), 256)
                got = jnp.dot(vs[plane, rows, :], perm[q], preferred_element_type=F32)
                shf[q, rows, plane * PL:(plane + 1) * PL] = got

    lane_z = zz

    @pl.loop(0, 18)
    def _(k):
        for plane in range(2):
            for j in range(3):
                row = jnp.broadcast_to(lk[j * 18 + k, plane:plane + 1, :], (8, PL))
                if j == 1:
                    low = pltpu.roll(row, LZ, 1)
                elif j == 2:
                    low = jnp.where(lane_z == 0, pltpu.roll(row, PL - LZ + 1, 1), pltpu.roll(row, 1, 1))
                for lt in range(2):
                    sl = slice(lt * 128, lt * 128 + 128)
                    bc[plane * 2 + lt, j * 18 + k] = row[:, sl]
                    if j > 0:
                        bc[plane * 2 + lt, 54 + j * 18 + k] = low[:, sl]
                    elif plane == 0:
                        bc[2 + lt, 54 + k] = row[:, sl]

    z_copy.wait()
    st1 = 8 - 6 * core
    st2 = 2 + 6 * core
    p1 = cx * (1 - core) + cy * core
    p2 = cy * (1 - core) + cx * core

    def along(d, pos, stride):
        return me + (lax.rem(pos + d, 4) - pos) * stride

    gathers = []
    for d in range(1, 4):
        g = remote(tbuf.at[me], tbuf.at[me], s_g.at[d - 1], r_g1.at[d - 1], plane_dev(along(d, p1, st1)))
        g.start()
        gathers.append(g)
    sibs = [remote(tbuf.at[me], tbuf.at[me], s_g.at[15], r_sib, plane_dev(sib))]
    sibs[0].start()

    w_copy.wait()
    for plane in range(2):
        for r in range(24):
            w = jnp.broadcast_to(wloc[plane, r:r + 1, :] + wrem[plane, r:r + 1, :], (8, PL))
            for lt in range(2):
                bc[plane * 2 + lt, WROW + r] = w[:, lt * 128:lt * 128 + 128]

    for cp in halo:
        cp.wait()

    @pl.loop(0, 18)
    def _(k):
        row = jnp.broadcast_to(halo_l[k, 1:2, :], (8, PL))
        for lt in range(2):
            bc[lt, 54 + k] = row[:, lt * 128:lt * 128 + 128]

    def tile_work(t, vg):
        lanes = pl.ds(pl.multiple_of(t * 128, 128), 128)
        rows = pl.ds(pl.multiple_of(vg * 16, 16), 16)

        def field(j, back, f):
            if j == 0:
                ref = xm if back else xp
                return ref[f, rows, lanes].astype(F32).reshape(2, 8, 128)
            q = (j - 1) * 2 + back
            return shf[q, pl.ds(pl.multiple_of(f * NB + vg * 16, 16), 16), lanes].reshape(2, 8, 128)

        def coef(r):
            return bc[t, r][None]

        for c in range(3):
            acc = [[None, None] for _ in range(HEL)]
            for j in range(3):
                re = None
                im = None
                for c2 in range(3):
                    fr, fi = field(j, 0, c2), field(j, 0, 3 + c2)
                    gr, gi = field(j, 1, c2), field(j, 1, 3 + c2)
                    ur = coef(j * 18 + (c * 3 + c2) * 2)
                    ui = coef(j * 18 + (c * 3 + c2) * 2 + 1)
                    lr = coef(54 + j * 18 + (c2 * 3 + c) * 2)
                    li = coef(54 + j * 18 + (c2 * 3 + c) * 2 + 1)
                    a = ur * fr - ui * fi
                    b = ur * fi + ui * fr
                    a = a - lr * gr - li * gi
                    b = b - lr * gi + li * gr
                    re = a if re is None else re + a
                    im = b if im is None else im + b
                for h in range(HEL):
                    wr = coef(WROW + (h * 3 + j) * 2)
                    wi = coef(WROW + (h * 3 + j) * 2 + 1)
                    a = wr * re - wi * im
                    b = wr * im + wi * re
                    acc[h][0] = a if acc[h][0] is None else acc[h][0] + a
                    acc[h][1] = b if acc[h][1] is None else acc[h][1] + b
            cols = pl.ds(pl.multiple_of(c * 2 * PL + t * 128, 128), 128)
            for h in range(HEL):
                for ri in range(2):
                    dst = pl.ds(pl.multiple_of(ri * NB + vg * 16, 16), 16)
                    dbuf[h, dst, cols] = acc[h][ri].reshape(16, 128).astype(BF16)

    def run_tiles(t0, t1):
        @pl.loop(t0 * 8, t1 * 8)
        def _(i):
            tile_work(i // 8, lax.rem(i, 8))

    run_tiles(0, 2)

    for g in gathers:
        g.wait()
    second = []
    for a in range(4):
        k = along(a, p1, st1)
        for d in range(1, 4):
            where = k + (lax.rem(p2 + d, 4) - p2) * st2
            g = remote(tbuf.at[k], tbuf.at[k], s_g.at[3 + a * 3 + d - 1], r_g2.at[a * 3 + d - 1],
                       plane_dev(along(d, p2, st2)))
            del where
            g.start()
            second.append(g)
        if a > 0:
            s = remote(tbuf.at[k], tbuf.at[k], s_g.at[15], r_sib, plane_dev(sib))
            s.start()
            sibs.append(s)

    run_tiles(2, 4)

    @pl.loop(0, HEL)
    def _(h):
        full = nt_dot(v2[...], dbuf[h])
        re = full[:NV, :NB] + full[NV:, NB:]
        im = full[:NV, NB:] - full[NV:, :NB]
        pbuf[:, h, 0] = re.reshape(NS, 8, NB)
        pbuf[:, h, 1] = im.reshape(NS, 8, NB)

        @pl.loop(1, NS)
        def _(d):
            owner = lax.rem(me + d, NS)
            remote(pbuf.at[owner, h], rbuf.at[d - 1, h], s_rs, r_rs, plane_dev(owner)).start()

    for g in second:
        g.wait()
    for a in range(4):
        for d in range(1, 4):
            k = along(a, p1, st1) + (lax.rem(p2 + 4 - d, 4) - p2) * st2
            s = remote(tbuf.at[k], tbuf.at[k], s_g.at[15], r_sib, plane_dev(sib))
            s.start()
            sibs.append(s)

    whole = remote(pbuf.at[pl.ds(0, NS - 1)], rbuf, s_rs, r_rs, plane_dev(nxt))
    whole.wait_recv()

    def add(d, acc):
        return acc + rbuf[d]

    total = lax.fori_loop(0, NS - 1, add, pbuf[me])
    sbuf[...] = total.reshape(HEL, 16, NB).astype(BF16)
    mine = pl.ds(2 * op, 2)
    theirs = pl.ds(2 * (1 - op), 2)
    cols = pl.ds(pl.multiple_of(op * NB, NB), NB)
    o_copy = remote(sbuf.at[theirs], obuf.at[:, :, cols], s_o, r_o, dev(me, tm, 1 - op))
    o_copy.start()
    obuf[:, :, cols] = sbuf[mine]
    whole.wait_send()
    o_copy.wait()

    parity = remote(tbuf.at[pl.ds(0, 16)], tbuf.at[pl.ds(0, 16)], s_g.at[15], r_sib, plane_dev(sib))
    parity.wait()

    ops = obuf[...].astype(F32)
    lines = []
    for h in range(2):
        o_r, o_i = ops[h, 0:8], ops[h, 8:16]
        lines.append(jnp.concatenate([o_r, -o_i], 1))
        lines.append(jnp.concatenate([o_i, o_r], 1))
    left = jnp.concatenate(lines, 0).astype(BF16)

    @pl.loop(0, 16)
    def _(g):
        right = jnp.concatenate([tbuf[2 * g], tbuf[2 * g + 1]], 1)
        res = jnp.dot(left, right, preferred_element_type=F32)
        out[:, g] = res.reshape(2, 2, 8, NV)


def shards(eigvecs, links, momenta, coef_num, coef_den, peram):
    v2 = eigvecs[0].reshape(2 * NV, 3 * 2 * PL)
    lk = links[0].reshape(54, 2, PL)
    me = lax.axis_index("space")
    per = peram[0].reshape(NV, 16, 2, NV)
    piece = lax.dynamic_slice(per, (0, me // 2, 0, (me % 2) * 128), (NV, 1, 2, 128))
    piece = jnp.transpose(piece[:, 0], (1, 0, 2)).reshape(2 * NV, 128)
    vm = pl.BlockSpec(memory_space=pltpu.VMEM)
    sm = pl.BlockSpec(memory_space=pltpu.SMEM)
    dma = pltpu.SemaphoreType.DMA
    out = pl.pallas_call(
        kernel,
        out_shape=jax.ShapeDtypeStruct((2, 16, 2, 8, NV), F32),
        in_specs=[sm, sm, sm, vm, vm, vm],
        out_specs=vm,
        scratch_shapes=[
            pltpu.VMEM((6, NB, 2 * PL), BF16),
            pltpu.VMEM((6, NB, 2 * PL), BF16),
            pltpu.VMEM((18, 2, PL), F32),
            pltpu.VMEM((2, 24, PL), F32),
            pltpu.VMEM((2, 24, PL), F32),
            pltpu.VMEM((4, 132, 8, 128), F32),
            pltpu.VMEM((2, 6 * NB, PL), BF16),
            pltpu.VMEM((4, PL, PL), BF16),
            pltpu.VMEM((4, 6 * NB, 2 * PL), F32),
            pltpu.VMEM((HEL, NV, 6 * PL), BF16),
            pltpu.VMEM((NS, HEL, 2, 8, NB), F32),
            pltpu.VMEM((NS - 1, HEL, 2, 8, NB), F32),
            pltpu.VMEM((NS, 2 * NV, 128), BF16),
            pltpu.VMEM((HEL, 16, NB), BF16),
            pltpu.VMEM((2, 16, NV), BF16),
            dma((13,)), dma((6,)), dma((6,)), dma, dma, dma, dma, dma,
            dma((16,)), dma((3,)), dma((12,)), dma, dma, dma, dma, dma,
        ],
        compiler_params=pltpu.CompilerParams(collective_id=0, has_side_effects=True,
                                             vmem_limit_bytes=60 * 1024 * 1024),
    )(momenta, coef_num, coef_den, lk, v2, piece)
    return out.reshape(1, 2, 4, 4, 2, 8, NV)


def solution(mesh):
    return jax.shard_map(
        shards,
        mesh=mesh,
        in_specs=(
            P("tm", None, None, None, "space", None),
            P("tm", None, None, None, None, "space", None),
            P("op", None),
            P(None, "op", None),
            P(),
            P("tm", None, None, None, None, None),
        ),
        out_specs=P("tm", "op", None, None, None, "space", None),
        check_vma=False,
    )
```

profile of v0, /device:TPU:1, one launch (start us, length us, event | category | flops | bytes accessed | tf_op | source)
XLA Modules:
  0.0 63.3 jit_solution(1927469631534855717)
XLA Ops:
  0.0 1.4 %copy.8.num = s32[4,2,3]{2,1,0:T(2,128)} copy(s32[4,2,3]{0,1,2:T(2,128)} %param.9) | data formatting | bytes 192 | tf_op args[3]
  1.4 1.0 %constant_dynamic-slice_fusion = bf16[256,1,2,128]{3,2,1,0:T(2,128)(2,1)S(1)} fusion(bf16[256,16,2,256]{3,2,1,0:T(2,128)(2,1)} %bitcast.11, s32[]{:T(128)S(6)} %select_n.18, s32[]{:T(128)S(6)} %select_n.20), kind=kLoop, calls=%fused_computation | loop fusion | bytes 262152 | tf_op jit(solution)/shard_map/dynamic_slice | solution.py:315
  2.4 0.7 %copy.7 = bf16[256,1,2,128]{3,0,2,1:T(8,128)(2,1)} copy(bf16[256,1,2,128]{3,2,1,0:T(2,128)(2,1)S(1)} %constant_dynamic-slice_fusion) | data formatting | bytes 262144 | tf_op jit(solution)/shard_map/dynamic_slice | solution.py:315
  3.0 4.9 %reshape_squeeze.10.v2 = bf16[512,1536]{1,0:T(8,128)(2,1)} reshape(bf16[1,2,256,3,2,256]{5,4,3,2,1,0:T(2,128)(2,1)} %param.6) | data formatting | bytes 3145728 | tf_op jit(solution)/shard_map/reshape;squeeze | solution.py:311
  7.9 53.5 %shard_map.64 = f32[2,16,2,8,256]{4,3,2,1,0:T(8,128)} custom-call(s32[2,3]{1,0:T(2,128)} %mom.1, s32[4,2,3]{2,1,0:T(2,128)} %copy.8.num, s32[4]{0:T(128)} %den.1, f32[54,2,256]{2,1,0:T(2,128)} %bitcast.10, bf16[512,1536]{1,0:T(8,128)(2,1)} %reshape_squeeze.10.v2, bf16[512,128]{1,0:T(8,128)(2,1)} %bitcast.9), custom_call_target="tpu_custom_call" | custom-call | tf_op jit(solution)/shard_map/pallas_call | solution.py:320
  61.4 1.9 %copy.10 = f32[1,2,4,4,2,8,256]{6,5,4,3,2,1,0:T(8,128)} copy(f32[1,2,4,4,2,8,256]{6,5,4,3,2,1,0:T(8,128)} %bitcast.8) | data formatting | bytes 1048576
where the time goes:
time: 63.6 us; the launch traced here: 63.3 us
  Pallas kernels  53.5 us (84%)
  local copies, waits for them, and re-layouts  9.78 us (15%)
    pallas_call x1, Pallas kernels, shards(): pl.pallas_call(kernel, out_shape=jax.ShapeDtypeStruct((2, 16, 2, 8, NV),...  53.5 us
    another operation x1, local copies, waits for them, and re-layouts, shards(): v2 = eigvecs[0].reshape(2 * NV, 3 * 2 * PL)  4.88 us
    unnamed x2, local copies, waits for them, and re-layouts  3.23 us
    dynamic_slice x2, local copies, waits for them, and re-layouts, shards(): lax.dynamic_slice(per, (0, me // 2, 0, me % 2 * 128), (NV, 1, 2, 128))  1.67 us

commit v1 on v0

--- a/solution.py
+++ b/solution.py
@@ -27,9 +27,9 @@
     return lax.dot_general(a, b, (((1,), (1,)), ((), ())), preferred_element_type=F32)
 
 
-def kernel(mom, num, den, lk, v2, piece, out,
+def kernel(mom, num, den, lk, v, piece, out,
            xp, xm, halo_l, wloc, wrem, bc, vs, perm, shf, dbuf, pbuf, rbuf, tbuf, sbuf, obuf,
-           s_halo, r_up, r_dn, r_lk, s_w, r_w, s_z, r_z, s_g, r_g1, r_g2, r_sib, s_rs, r_rs, s_o, r_o):
+           s_halo, r_up, r_dn, r_lk, s_w, r_w, s_z, r_z, s_g, r_g1, r_g2, s_sib, r_sib, s_rs, r_rs, s_o, r_o):
     me = lax.axis_index("space")
     tm = lax.axis_index("tm")
     op = lax.axis_index("op")
@@ -52,6 +52,24 @@
     nxt = lax.rem(me + 1, NS)
     prv = lax.rem(me + NS - 1, NS)
 
+    st1 = 8 - 6 * core
+    st2 = 2 + 6 * core
+    p1 = cx * (1 - core) + cy * core
+    p2 = cy * (1 - core) + cx * core
+    LOW, HIGH, ALL = pl.ds(0, NV), pl.ds(NV, NV), pl.ds(0, 2 * NV)
+
+    def move1(s, d):
+        return s + (lax.rem(p1 + d, 4) - p1) * st1
+
+    def move2(s, d):
+        return s + (lax.rem(p2 + d, 4) - p2) * st2
+
+    def held(s, o):
+        return move2(s, 2 * o)
+
+    right1, left1 = move1(me, 1), move1(me, 3)
+    right2, left2 = move2(me, 1), move2(me, 3)
+
     barrier = pltpu.get_barrier_semaphore()
 
     @pl.loop(1, NS)
@@ -60,30 +78,10 @@
 
     pl.semaphore_signal(barrier, inc=1, device_id=dev(me, tm, 1 - op), device_id_type=MESH)
     pl.semaphore_signal(barrier, inc=1, device_id=dev(me, 1 - tm, 1 - op), device_id_type=MESH)
-    pl.semaphore_wait(barrier, NS + 1)
-
-    z_copy = remote(piece, tbuf.at[me], s_z, r_z, dev(me, 1 - tm, 1 - op))
-    z_copy.start()
-
-    brow = pl.multiple_of(op * NB, NB)
-    halo = []
-    for f in range(6):
-        ri, c = f // 3, f % 3
-        rows = pl.ds(pl.multiple_of(ri * NV + brow, NB), NB)
-        up = remote(v2.at[rows, pl.ds(c * 2 * PL, PL)], xp.at[f, :, pl.ds(PL, PL)],
-                    s_halo.at[f], r_up.at[f], plane_dev(prv))
-        dn = remote(v2.at[rows, pl.ds(c * 2 * PL + PL, PL)], xm.at[f, :, pl.ds(0, PL)],
-                    s_halo.at[6 + f], r_dn.at[f], plane_dev(nxt))
-        up.start()
-        dn.start()
-        halo += [up, dn]
-    lk_copy = remote(lk.at[pl.ds(0, 18)], halo_l, s_halo.at[12], r_lk, plane_dev(nxt))
-    lk_copy.start()
-    halo.append(lk_copy)
 
     site = lax.broadcasted_iota(jnp.int32, (8, PL), 1)
     yy = site // LZ
-    zz = lax.rem(site, LZ)
+    zz = site & (LZ - 1)
     inv = [SCALE / (jnp.zeros((8, PL), F32) + den[h].astype(F32)) for h in range(HEL)]
     for plane in range(2):
         phase = []
@@ -94,24 +92,44 @@
             phase.append((jnp.cos(theta), -jnp.sin(theta)))
         for h in range(HEL):
             for j in range(3):
-                n0 = num[h, 0, j].astype(F32)
-                n1 = num[h, 1, j].astype(F32)
+                n0 = num[j, 0, h].astype(F32)
+                n1 = num[j, 1, h].astype(F32)
                 for ri in range(2):
                     w = (phase[0][ri] * n0 + phase[1][ri] * n1) * inv[h]
                     row = (h * 3 + j) * 2 + ri
                     wloc[plane, row:row + 1, :] = w[0:1]
+
+    pl.semaphore_wait(barrier, NS + 1)
+
+    z_copy = remote(piece, tbuf.at[held(me, 1 - op)], s_z, r_z, dev(me, 1 - tm, 1 - op))
+    came = held(me, op)
+    z_copy.start()
+
+    brow = pl.ds(pl.multiple_of(op * NB, NB), NB)
+    halo = []
+    for f in range(6):
+        ri, c = f // 3, f % 3
+        up = remote(v.at[c, 0, ri, brow], xp.at[f, :, pl.ds(PL, PL)],
+                    s_halo.at[f], r_up.at[f], plane_dev(prv))
+        dn = remote(v.at[c, 1, ri, brow], xm.at[f, :, pl.ds(0, PL)],
+                    s_halo.at[6 + f], r_dn.at[f], plane_dev(nxt))
+        up.start()
+        dn.start()
+        halo += [up, dn]
+    lk_copy = remote(lk.at[pl.ds(0, 18)], halo_l, s_halo.at[12], r_lk, plane_dev(nxt))
+    lk_copy.start()
+    halo.append(lk_copy)
     w_copy = remote(wloc, wrem, s_w, r_w, dev(me, tm, 1 - op))
     w_copy.start()
 
     for f in range(6):
         ri, c = f // 3, f % 3
-        rows = pl.ds(pl.multiple_of(ri * NV + brow, NB), NB)
-        p0 = v2[rows, c * 2 * PL:c * 2 * PL + PL]
-        p1 = v2[rows, c * 2 * PL + PL:(c + 1) * 2 * PL]
-        xp[f, :, 0:PL] = p1
-        xm[f, :, PL:2 * PL] = p0
-        vs[0, f * NB:(f + 1) * NB, :] = p0
-        vs[1, f * NB:(f + 1) * NB, :] = p1
+        even = v[c, 0, ri, brow]
+        odd = v[c, 1, ri, brow]
+        xp[f, :, 0:PL] = odd
+        xm[f, :, PL:2 * PL] = even
+        vs[0, f * NB:(f + 1) * NB, :] = even
+        vs[1, f * NB:(f + 1) * NB, :] = odd
     r_i = lax.broadcasted_iota(jnp.int32, (PL, PL), 0)
     c_i = lax.broadcasted_iota(jnp.int32, (PL, PL), 1)
     zc = c_i & (LZ - 1)
@@ -121,13 +139,32 @@
         perm[q] = jnp.where(r_i == sources[q], 1.0, 0.0).astype(BF16)
     for q in range(4):
         for plane in range(2):
-            @pl.loop(0, 3)
-            def _(m):
-                rows = pl.ds(pl.multiple_of(m * 256, 256), 256)
-                got = jnp.dot(vs[plane, rows, :], perm[q], preferred_element_type=F32)
-                shf[q, rows, plane * PL:(plane + 1) * PL] = got
-
-    lane_z = zz
+            shf[q, :, plane * PL:(plane + 1) * PL] = jnp.dot(vs[plane], perm[q], preferred_element_type=F32)
+
+    z_copy.wait()
+    def send(k, part, n, rsem, where):
+        ref = tbuf.at[k, part]
+        g = remote(ref, ref, s_g.at[n], rsem, plane_dev(where))
+        g.start()
+        return g
+
+    def to_sibling(k):
+        ref = tbuf.at[k]
+        remote(ref, ref, s_sib, r_sib, plane_dev(sib)).start()
+
+    def spread(k, n):
+        ahead.append((send(k, ALL, 4 + 2 * n, r_g2.at[2 * n], right2),
+                      send(k, ALL, 5 + 2 * n, r_g2.at[2 * n + 1], left2)))
+        ref = tbuf.at[k]
+        g = remote(ref, ref, s_g.at[12 + n], r_g2.at[8 + n], dev(me, tm, 1 - op))
+        g.start()
+        across.append(g)
+        to_sibling(k)
+
+    ahead = []
+    across = []
+    first = [send(came, ALL, 0, r_g1.at[0], right1), send(came, ALL, 1, r_g1.at[1], left1)]
+    spread(came, 0)
 
     @pl.loop(0, 18)
     def _(k):
@@ -137,7 +174,7 @@
                 if j == 1:
                     low = pltpu.roll(row, LZ, 1)
                 elif j == 2:
-                    low = jnp.where(lane_z == 0, pltpu.roll(row, PL - LZ + 1, 1), pltpu.roll(row, 1, 1))
+                    low = jnp.where(zz == 0, pltpu.roll(row, PL - LZ + 1, 1), pltpu.roll(row, 1, 1))
                 for lt in range(2):
                     sl = slice(lt * 128, lt * 128 + 128)
                     bc[plane * 2 + lt, j * 18 + k] = row[:, sl]
@@ -145,23 +182,6 @@
                         bc[plane * 2 + lt, 54 + j * 18 + k] = low[:, sl]
                     elif plane == 0:
                         bc[2 + lt, 54 + k] = row[:, sl]
-
-    z_copy.wait()
-    st1 = 8 - 6 * core
-    st2 = 2 + 6 * core
-    p1 = cx * (1 - core) + cy * core
-    p2 = cy * (1 - core) + cx * core
-
-    def along(d, pos, stride):
-        return me + (lax.rem(pos + d, 4) - pos) * stride
-
-    gathers = []
-    for d in range(1, 4):
-        g = remote(tbuf.at[me], tbuf.at[me], s_g.at[d - 1], r_g1.at[d - 1], plane_dev(along(d, p1, st1)))
-        g.start()
-        gathers.append(g)
-    sibs = [remote(tbuf.at[me], tbuf.at[me], s_g.at[15], r_sib, plane_dev(sib))]
-    sibs[0].start()
 
     w_copy.wait()
     for plane in range(2):
@@ -224,62 +244,71 @@
                     dst = pl.ds(pl.multiple_of(ri * NB + vg * 16, 16), 16)
                     dbuf[h, dst, cols] = acc[h][ri].reshape(16, 128).astype(BF16)
 
-    def run_tiles(t0, t1):
-        @pl.loop(t0 * 8, t1 * 8)
+    def run_tiles(i0, i1):
+        @pl.loop(i0, i1)
         def _(i):
             tile_work(i // 8, lax.rem(i, 8))
 
-    run_tiles(0, 2)
-
-    for g in gathers:
+    run_tiles(0, 8)
+
+    for g in first:
         g.wait()
-    second = []
-    for a in range(4):
-        k = along(a, p1, st1)
-        for d in range(1, 4):
-            where = k + (lax.rem(p2 + d, 4) - p2) * st2
-            g = remote(tbuf.at[k], tbuf.at[k], s_g.at[3 + a * 3 + d - 1], r_g2.at[a * 3 + d - 1],
-                       plane_dev(along(d, p2, st2)))
-            del where
-            g.start()
-            second.append(g)
-        if a > 0:
-            s = remote(tbuf.at[k], tbuf.at[k], s_g.at[15], r_sib, plane_dev(sib))
-            s.start()
-            sibs.append(s)
-
-    run_tiles(2, 4)
+    kl, kr, ko = move1(came, 3), move1(came, 1), move1(came, 2)
+    onward = [send(kl, LOW, 2, r_g1.at[2], right1), send(kr, HIGH, 3, r_g1.at[3], left1)]
+    spread(kl, 1)
+    spread(kr, 2)
+
+    run_tiles(8, 16)
+
+    for g in onward:
+        g.wait()
+    spread(ko, 3)
+
+    run_tiles(16, 24)
+
+    def settle(n):
+        for g in ahead[n]:
+            g.wait()
+        across[n].wait()
+        k = (came, kl, kr, ko)[n]
+        to_sibling(turned(k, 3))
+        to_sibling(turned(k, 1))
+        to_sibling(turned(k, 2))
+
+    def turned(k, d):
+        at = lax.rem(p2 + 2 * op, 4)
+        return k + (lax.rem(at + d, 4) - at) * st2
+
+    settle(0)
+    run_tiles(24, 32)
 
     @pl.loop(0, HEL)
     def _(h):
-        full = nt_dot(v2[...], dbuf[h])
+        full = None
+        for cp in range(6):
+            part = nt_dot(v[cp // 2, cp % 2].reshape(2 * NV, PL), dbuf[h, :, cp * PL:(cp + 1) * PL])
+            full = part if full is None else full + part
         re = full[:NV, :NB] + full[NV:, NB:]
         im = full[:NV, NB:] - full[NV:, :NB]
-        pbuf[:, h, 0] = re.reshape(NS, 8, NB)
-        pbuf[:, h, 1] = im.reshape(NS, 8, NB)
+        both = jnp.concatenate([re.reshape(NS, 8, NB), im.reshape(NS, 8, NB)], 1)
+        pbuf[:, h] = both.astype(BF16)
 
         @pl.loop(1, NS)
         def _(d):
             owner = lax.rem(me + d, NS)
             remote(pbuf.at[owner, h], rbuf.at[d - 1, h], s_rs, r_rs, plane_dev(owner)).start()
 
-    for g in second:
-        g.wait()
-    for a in range(4):
-        for d in range(1, 4):
-            k = along(a, p1, st1) + (lax.rem(p2 + 4 - d, 4) - p2) * st2
-            s = remote(tbuf.at[k], tbuf.at[k], s_g.at[15], r_sib, plane_dev(sib))
-            s.start()
-            sibs.append(s)
+    for n in range(1, 4):
+        settle(n)
 
     whole = remote(pbuf.at[pl.ds(0, NS - 1)], rbuf, s_rs, r_rs, plane_dev(nxt))
     whole.wait_recv()
 
     def add(d, acc):
-        return acc + rbuf[d]
-
-    total = lax.fori_loop(0, NS - 1, add, pbuf[me])
-    sbuf[...] = total.reshape(HEL, 16, NB).astype(BF16)
+        return acc + rbuf[d].astype(F32)
+
+    total = lax.fori_loop(0, NS - 1, add, pbuf[me].astype(F32))
+    sbuf[...] = total.astype(BF16)
     mine = pl.ds(2 * op, 2)
     theirs = pl.ds(2 * (1 - op), 2)
     cols = pl.ds(pl.multiple_of(op * NB, NB), NB)
@@ -289,8 +318,8 @@
     whole.wait_send()
     o_copy.wait()
 
-    parity = remote(tbuf.at[pl.ds(0, 16)], tbuf.at[pl.ds(0, 16)], s_g.at[15], r_sib, plane_dev(sib))
-    parity.wait()
+    half = tbuf.at[pl.ds(0, 16)]
+    remote(half, half, s_sib, r_sib, plane_dev(sib)).wait()
 
     ops = obuf[...].astype(F32)
     lines = []
@@ -308,11 +337,16 @@
 
 
 def shards(eigvecs, links, momenta, coef_num, coef_den, peram):
-    v2 = eigvecs[0].reshape(2 * NV, 3 * 2 * PL)
+    v = jnp.transpose(eigvecs[0], (2, 3, 0, 1, 4))
     lk = links[0].reshape(54, 2, PL)
     me = lax.axis_index("space")
+    core = me % 2
+    row = 2 * lax.axis_index("op")
+    cx, cy = me // 8, (me // 2) % 4
+    row = 2 - row
+    place = jnp.where(core == 0, cx * 4 + (cy + row) % 4, (cx + row) % 4 * 4 + cy)
     per = peram[0].reshape(NV, 16, 2, NV)
-    piece = lax.dynamic_slice(per, (0, me // 2, 0, (me % 2) * 128), (NV, 1, 2, 128))
+    piece = lax.dynamic_slice(per, (0, place, 0, core * 128), (NV, 1, 2, 128))
     piece = jnp.transpose(piece[:, 0], (1, 0, 2)).reshape(2 * NV, 128)
     vm = pl.BlockSpec(memory_space=pltpu.VMEM)
     sm = pl.BlockSpec(memory_space=pltpu.SMEM)
@@ -333,17 +367,17 @@
             pltpu.VMEM((4, PL, PL), BF16),
             pltpu.VMEM((4, 6 * NB, 2 * PL), F32),
             pltpu.VMEM((HEL, NV, 6 * PL), BF16),
-            pltpu.VMEM((NS, HEL, 2, 8, NB), F32),
-            pltpu.VMEM((NS - 1, HEL, 2, 8, NB), F32),
+            pltpu.VMEM((NS, HEL, 16, NB), BF16),
+            pltpu.VMEM((NS - 1, HEL, 16, NB), BF16),
             pltpu.VMEM((NS, 2 * NV, 128), BF16),
             pltpu.VMEM((HEL, 16, NB), BF16),
             pltpu.VMEM((2, 16, NV), BF16),
             dma((13,)), dma((6,)), dma((6,)), dma, dma, dma, dma, dma,
-            dma((16,)), dma((3,)), dma((12,)), dma, dma, dma, dma, dma,
+            dma((20,)), dma((4,)), dma((16,)), dma, dma, dma, dma, dma, dma,
         ],
         compiler_params=pltpu.CompilerParams(collective_id=0, has_side_effects=True,
                                              vmem_limit_bytes=60 * 1024 * 1024),
-    )(momenta, coef_num, coef_den, lk, v2, piece)
+    )(momenta, jnp.transpose(coef_num, (2, 1, 0)), coef_den, lk, v, piece)
     return out.reshape(1, 2, 4, 4, 2, 8, NV)
 
 

time: 63.6 us -> 49.3 us (0.78)
  Pallas kernels: 53.5 us -> 42.7 us
  local copies, waits for them, and re-layouts: 9.78 us -> 6.33 us
    pallas_call x1, Pallas kernels: 53.5 us -> 42.7 us  [shards(): pl.pallas_call(kernel, out_shape=jax.ShapeDtypeStruct((2, 16, 2, 8, NV),...]
    another operation x1 -> x0, local copies, waits for them, and re-layouts: 4.88 us -> none  [shards(): v2 = eigvecs[0].reshape(2 * NV, 3 * 2 * PL)]
    unnamed x2, local copies, waits for them, and re-layouts: 3.23 us -> 4.66 us
where the time goes in v1:
time: 49.3 us; the launch traced here: 49.1 us
  Pallas kernels  42.7 us (87%)
  local copies, waits for them, and re-layouts  6.33 us (13%)
    pallas_call x1, Pallas kernels, shards(): pl.pallas_call(kernel, out_shape=jax.ShapeDtypeStruct((2, 16, 2, 8, NV),...  42.7 us
    unnamed x2, local copies, waits for them, and re-layouts  4.66 us
    dynamic_slice x2, local copies, waits for them, and re-layouts, shards(): piece = lax.dynamic_slice(per, (0, place, 0, core * 128), (NV, 1, 2, 128))  1.67 us

profile of v1, /device:TPU:1, one launch (start us, length us, event | category | flops | bytes accessed | tf_op | source)
XLA Modules:
  0.0 49.1 jit_solution(6314145686206030970)
XLA Ops:
  0.0 1.0 %constant_dynamic-slice_fusion = bf16[256,1,2,128]{3,2,1,0:T(2,128)(2,1)S(1)} fusion(bf16[256,16,2,256]{3,2,1,0:T(2,128)(2,1)} %bitcast.18, s32[]{:T(128)S(6)} %select_n.42, s32[]{:T(128)S(6)} %select_n.43), kind=kLoop, calls=%fused_computation.1 | loop fusion | bytes 262152 | tf_op jit(solution)/shard_map/dynamic_slice | solution.py:349
  1.0 0.7 %copy.8 = bf16[256,1,2,128]{3,0,2,1:T(8,128)(2,1)} copy(bf16[256,1,2,128]{3,2,1,0:T(2,128)(2,1)S(1)} %constant_dynamic-slice_fusion) | data formatting | bytes 262144 | tf_op jit(solution)/shard_map/dynamic_slice | solution.py:349
  1.7 2.8 %copy.10 = bf16[1,2,256,3,2,256]{5,2,1,4,3,0:T(8,128)(2,1)} copy(bf16[1,2,256,3,2,256]{5,4,3,2,1,0:T(2,128)(2,1)} %param.6) | data formatting | bytes 3145728 | tf_op args[0]
  4.5 42.7 %shard_map.64 = f32[2,16,2,8,256]{4,3,2,1,0:T(8,128)} custom-call(s32[2,3]{1,0:T(2,128)} %mom.1, s32[3,2,4]{2,1,0:T(2,128)} %bitcast.19, s32[4]{0:T(128)} %den.1, f32[54,2,256]{2,1,0:T(2,128)} %bitcast.17, bf16[3,2,2,256,256]{4,3,2,1,0:T(8,128)(2,1)} %bitcast.14, bf16[512,128]{1,0:T(8,128)(2,1)} %bitcast.16), custom_call_target="tpu_custom_call" | custom-call | tf_op jit(solution)/shard_map/pallas_call | solution.py:354
  47.2 1.9 %copy.12 = f32[1,2,4,4,2,8,256]{6,5,4,3,2,1,0:T(8,128)} copy(f32[1,2,4,4,2,8,256]{6,5,4,3,2,1,0:T(8,128)} %bitcast.15) | data formatting | bytes 1048576

commit v2 on v1

--- a/solution.py
+++ b/solution.py
@@ -28,8 +28,8 @@
 
 
 def kernel(mom, num, den, lk, v, piece, out,
-           xp, xm, halo_l, wloc, wrem, bc, vs, perm, shf, dbuf, pbuf, rbuf, tbuf, sbuf, obuf,
-           s_halo, r_up, r_dn, r_lk, s_w, r_w, s_z, r_z, s_g, r_g1, r_g2, s_sib, r_sib, s_rs, r_rs, s_o, r_o):
+           xp, xm, halo_l, wloc, wrem, bc, vs, perm, shf, part, dbuf, pf, pq, ps, pbuf, rbuf, tbuf, sbuf, obuf,
+           s_halo, r_up, r_dn, r_lk, s_w, r_w, s_z, r_z, s_g, r_g1, r_g2, s_sib, r_sib, s_ps, r_ps, s_rs, r_rs, s_o, r_o):
     me = lax.axis_index("space")
     tm = lax.axis_index("tm")
     op = lax.axis_index("op")
@@ -72,12 +72,16 @@
 
     barrier = pltpu.get_barrier_semaphore()
 
-    @pl.loop(1, NS)
+    def same_core(d):
+        return lax.rem(chip + d, NS // 2) * 2 + core
+
+    @pl.loop(1, NS // 2)
     def _(d):
-        pl.semaphore_signal(barrier, inc=1, device_id=plane_dev(lax.rem(me + d, NS)), device_id_type=MESH)
-
-    pl.semaphore_signal(barrier, inc=1, device_id=dev(me, tm, 1 - op), device_id_type=MESH)
-    pl.semaphore_signal(barrier, inc=1, device_id=dev(me, 1 - tm, 1 - op), device_id_type=MESH)
+        pl.semaphore_signal(barrier, inc=1, device_id=plane_dev(same_core(d)), device_id_type=MESH)
+
+    cross = lax.rem(me + NS + 2 * core - 1, NS)
+    for where in (plane_dev(cross), plane_dev(sib), dev(me, tm, 1 - op), dev(me, 1 - tm, 1 - op)):
+        pl.semaphore_signal(barrier, inc=1, device_id=where, device_id_type=MESH)
 
     site = lax.broadcasted_iota(jnp.int32, (8, PL), 1)
     yy = site // LZ
@@ -99,11 +103,7 @@
                     row = (h * 3 + j) * 2 + ri
                     wloc[plane, row:row + 1, :] = w[0:1]
 
-    pl.semaphore_wait(barrier, NS + 1)
-
-    z_copy = remote(piece, tbuf.at[held(me, 1 - op)], s_z, r_z, dev(me, 1 - tm, 1 - op))
-    came = held(me, op)
-    z_copy.start()
+    pl.semaphore_wait(barrier, NS // 2 + 3)
 
     brow = pl.ds(pl.multiple_of(op * NB, NB), NB)
     halo = []
@@ -121,6 +121,10 @@
     halo.append(lk_copy)
     w_copy = remote(wloc, wrem, s_w, r_w, dev(me, tm, 1 - op))
     w_copy.start()
+
+    z_copy = remote(piece, tbuf.at[held(me, 1 - op)], s_z, r_z, dev(me, 1 - tm, 1 - op))
+    came = held(me, op)
+    z_copy.start()
 
     for f in range(6):
         ri, c = f // 3, f % 3
@@ -141,31 +145,6 @@
         for plane in range(2):
             shf[q, :, plane * PL:(plane + 1) * PL] = jnp.dot(vs[plane], perm[q], preferred_element_type=F32)
 
-    z_copy.wait()
-    def send(k, part, n, rsem, where):
-        ref = tbuf.at[k, part]
-        g = remote(ref, ref, s_g.at[n], rsem, plane_dev(where))
-        g.start()
-        return g
-
-    def to_sibling(k):
-        ref = tbuf.at[k]
-        remote(ref, ref, s_sib, r_sib, plane_dev(sib)).start()
-
-    def spread(k, n):
-        ahead.append((send(k, ALL, 4 + 2 * n, r_g2.at[2 * n], right2),
-                      send(k, ALL, 5 + 2 * n, r_g2.at[2 * n + 1], left2)))
-        ref = tbuf.at[k]
-        g = remote(ref, ref, s_g.at[12 + n], r_g2.at[8 + n], dev(me, tm, 1 - op))
-        g.start()
-        across.append(g)
-        to_sibling(k)
-
-    ahead = []
-    across = []
-    first = [send(came, ALL, 0, r_g1.at[0], right1), send(came, ALL, 1, r_g1.at[1], left1)]
-    spread(came, 0)
-
     @pl.loop(0, 18)
     def _(k):
         for plane in range(2):
@@ -190,16 +169,11 @@
             for lt in range(2):
                 bc[plane * 2 + lt, WROW + r] = w[:, lt * 128:lt * 128 + 128]
 
-    for cp in halo:
-        cp.wait()
-
-    @pl.loop(0, 18)
-    def _(k):
-        row = jnp.broadcast_to(halo_l[k, 1:2, :], (8, PL))
-        for lt in range(2):
-            bc[lt, 54 + k] = row[:, lt * 128:lt * 128 + 128]
-
-    def tile_work(t, vg):
+    def tile_work(i, dirs, load, store):
+        half = i // 16
+        t = lax.rem(i, 16) // 4
+        quarter = lax.rem(i, 4)
+        vg = half * 4 + quarter
         lanes = pl.ds(pl.multiple_of(t * 128, 128), 128)
         rows = pl.ds(pl.multiple_of(vg * 16, 16), 16)
 
@@ -215,7 +189,9 @@
 
         for c in range(3):
             acc = [[None, None] for _ in range(HEL)]
-            for j in range(3):
+            if load:
+                acc = [[part[i, (c * HEL + h) * 2 + ri] for ri in range(2)] for h in range(HEL)]
+            for j in dirs:
                 re = None
                 im = None
                 for c2 in range(3):
@@ -238,18 +214,90 @@
                     b = wr * im + wi * re
                     acc[h][0] = a if acc[h][0] is None else acc[h][0] + a
                     acc[h][1] = b if acc[h][1] is None else acc[h][1] + b
+            if not store:
+                for h in range(HEL):
+                    for ri in range(2):
+                        part[i, (c * HEL + h) * 2 + ri] = acc[h][ri]
+                continue
             cols = pl.ds(pl.multiple_of(c * 2 * PL + t * 128, 128), 128)
             for h in range(HEL):
                 for ri in range(2):
-                    dst = pl.ds(pl.multiple_of(ri * NB + vg * 16, 16), 16)
-                    dbuf[h, dst, cols] = acc[h][ri].reshape(16, 128).astype(BF16)
-
-    def run_tiles(i0, i1):
+                    dst = pl.ds(pl.multiple_of(ri * NB + h % 2 * (NB // 2) + quarter * 16, 16), 16)
+                    dbuf[half, h // 2, dst, cols] = acc[h][ri].reshape(16, 128).astype(BF16)
+
+    def run_tiles(i0, i1, dirs=(0, 1, 2), load=False, store=True):
         @pl.loop(i0, i1)
         def _(i):
-            tile_work(i // 8, lax.rem(i, 8))
-
-    run_tiles(0, 8)
+            tile_work(i, dirs, load, store)
+
+    def send(k, part, n, rsem, where):
+        ref = tbuf.at[k, part]
+        g = remote(ref, ref, s_g.at[n], rsem, plane_dev(where))
+        g.start()
+        return g
+
+    def to_sibling(k):
+        ref = tbuf.at[k]
+        remote(ref, ref, s_sib, r_sib, plane_dev(sib)).start()
+
+    def spread(k, n):
+        ahead.append((send(k, ALL, 4 + 2 * n, r_g2.at[2 * n], right2),
+                      send(k, ALL, 5 + 2 * n, r_g2.at[2 * n + 1], left2)))
+        ref = tbuf.at[k]
+        g = remote(ref, ref, s_g.at[12 + n], r_g2.at[8 + n], dev(me, tm, 1 - op))
+        g.start()
+        across.append(g)
+        to_sibling(k)
+
+    EARLY = 16
+    run_tiles(0, EARLY // 2, (1, 2), False, False)
+
+    z_copy.wait()
+    ahead = []
+    across = []
+    first = [send(came, ALL, 0, r_g1.at[0], right1), send(came, ALL, 1, r_g1.at[1], left1)]
+    spread(came, 0)
+
+    run_tiles(EARLY // 2, EARLY, (1, 2), False, False)
+
+    for cp in halo:
+        cp.wait()
+
+    @pl.loop(0, 18)
+    def _(k):
+        row = jnp.broadcast_to(halo_l[k, 1:2, :], (8, PL))
+        for lt in range(2):
+            bc[lt, 54 + k] = row[:, lt * 128:lt * 128 + 128]
+
+    run_tiles(0, EARLY, (0,), True, True)
+
+    def products(half):
+        for hp in range(2):
+            full = None
+            for cp in range(6):
+                prod = nt_dot(v[cp // 2, cp % 2].reshape(2 * NV, PL), dbuf[half, hp, :, cp * PL:(cp + 1) * PL])
+                full = prod if full is None else full + prod
+            re = full[:NV, :NB] + full[NV:, NB:]
+            im = full[:NV, NB:] - full[NV:, :NB]
+            pf[half, hp, :, :, 0:8] = re.reshape(NS // 2, 2, 8, NB)
+            pf[half, hp, :, :, 8:16] = im.reshape(NS // 2, 2, 8, NB)
+            pq[half, hp] = pf[half, hp, :, 1 - core].astype(BF16)
+        g = remote(pq.at[half], ps.at[half], s_ps.at[half], r_ps.at[half], plane_dev(sib))
+        g.start()
+        return g
+
+    def combine(half, g):
+        g.wait()
+        for hp in range(2):
+            pbuf[:, 2 * half + hp] = (pf[half, hp, :, core] + ps[half, hp].astype(F32)).astype(BF16)
+
+        @pl.loop(1, NS // 2)
+        def _(d):
+            owner = lax.rem(chip + d, NS // 2)
+            remote(pbuf.at[owner, pl.ds(2 * half, 2)], rbuf.at[d - 1, pl.ds(2 * half, 2)], s_rs, r_rs,
+                   plane_dev(owner * 2 + core)).start()
+
+    early = products(0)
 
     for g in first:
         g.wait()
@@ -258,13 +306,17 @@
     spread(kl, 1)
     spread(kr, 2)
 
-    run_tiles(8, 16)
+    run_tiles(EARLY, 22)
+    combine(0, early)
+    run_tiles(22, 27)
 
     for g in onward:
         g.wait()
     spread(ko, 3)
 
-    run_tiles(16, 24)
+    def turned(k, d):
+        at = lax.rem(p2 + 2 * op, 4)
+        return k + (lax.rem(at + d, 4) - at) * st2
 
     def settle(n):
         for g in ahead[n]:
@@ -275,65 +327,52 @@
         to_sibling(turned(k, 1))
         to_sibling(turned(k, 2))
 
-    def turned(k, d):
-        at = lax.rem(p2 + 2 * op, 4)
-        return k + (lax.rem(at + d, 4) - at) * st2
-
-    settle(0)
-    run_tiles(24, 32)
-
-    @pl.loop(0, HEL)
-    def _(h):
-        full = None
-        for cp in range(6):
-            part = nt_dot(v[cp // 2, cp % 2].reshape(2 * NV, PL), dbuf[h, :, cp * PL:(cp + 1) * PL])
-            full = part if full is None else full + part
-        re = full[:NV, :NB] + full[NV:, NB:]
-        im = full[:NV, NB:] - full[NV:, :NB]
-        both = jnp.concatenate([re.reshape(NS, 8, NB), im.reshape(NS, 8, NB)], 1)
-        pbuf[:, h] = both.astype(BF16)
-
-        @pl.loop(1, NS)
-        def _(d):
-            owner = lax.rem(me + d, NS)
-            remote(pbuf.at[owner, h], rbuf.at[d - 1, h], s_rs, r_rs, plane_dev(owner)).start()
-
-    for n in range(1, 4):
+    run_tiles(27, 32)
+    combine(1, products(1))
+
+    for n in range(4):
         settle(n)
 
-    whole = remote(pbuf.at[pl.ds(0, NS - 1)], rbuf, s_rs, r_rs, plane_dev(nxt))
+    whole = remote(pbuf.at[pl.ds(0, NS // 2 - 1)], rbuf, s_rs, r_rs, plane_dev(sib))
     whole.wait_recv()
 
     def add(d, acc):
         return acc + rbuf[d].astype(F32)
 
-    total = lax.fori_loop(0, NS - 1, add, pbuf[me].astype(F32))
-    sbuf[...] = total.astype(BF16)
-    mine = pl.ds(2 * op, 2)
-    theirs = pl.ds(2 * (1 - op), 2)
-    cols = pl.ds(pl.multiple_of(op * NB, NB), NB)
-    o_copy = remote(sbuf.at[theirs], obuf.at[:, :, cols], s_o, r_o, dev(me, tm, 1 - op))
+    own = pf[:, :, chip, core] + ps[:, :, chip].astype(F32)
+    total = lax.fori_loop(0, NS // 2 - 1, add, own.reshape(4, 16, NB))
+    sbuf[...] = total.reshape(2, 2, 16, NB).astype(BF16)
+    o_copy = remote(sbuf.at[:, 1 - op], obuf.at[op], s_o, r_o, dev(me, tm, 1 - op))
     o_copy.start()
-    obuf[:, :, cols] = sbuf[mine]
+    obuf[op] = sbuf[:, op]
     whole.wait_send()
     o_copy.wait()
 
     half = tbuf.at[pl.ds(0, 16)]
     remote(half, half, s_sib, r_sib, plane_dev(sib)).wait()
 
-    ops = obuf[...].astype(F32)
+    lane = lax.broadcasted_iota(jnp.int32, (16, NB), 1)
+    low = lane < NB // 2
+    rows = [[], []]
+    for o in range(2):
+        a, b = obuf[o, 0].astype(F32), obuf[o, 1].astype(F32)
+        rows[0].append(jnp.where(low, a, pltpu.roll(b, NB // 2, 1)))
+        rows[1].append(jnp.where(low, pltpu.roll(a, NB // 2, 1), b))
     lines = []
     for h in range(2):
-        o_r, o_i = ops[h, 0:8], ops[h, 8:16]
+        ops = jnp.concatenate(rows[h], 1)
+        o_r, o_i = ops[0:8], ops[8:16]
         lines.append(jnp.concatenate([o_r, -o_i], 1))
         lines.append(jnp.concatenate([o_i, o_r], 1))
     left = jnp.concatenate(lines, 0).astype(BF16)
 
-    @pl.loop(0, 16)
-    def _(g):
-        right = jnp.concatenate([tbuf[2 * g], tbuf[2 * g + 1]], 1)
-        res = jnp.dot(left, right, preferred_element_type=F32)
-        out[:, g] = res.reshape(2, 2, 8, NV)
+    @pl.loop(0, 4)
+    def _(q):
+        for n in range(4):
+            g = 4 * q + n
+            right = jnp.concatenate([tbuf[2 * g], tbuf[2 * g + 1]], 1)
+            res = jnp.dot(left, right, preferred_element_type=F32)
+            out[:, g] = res.reshape(2, 2, 8, NV)
 
 
 def shards(eigvecs, links, momenta, coef_num, coef_den, peram):
@@ -366,17 +405,21 @@
             pltpu.VMEM((2, 6 * NB, PL), BF16),
             pltpu.VMEM((4, PL, PL), BF16),
             pltpu.VMEM((4, 6 * NB, 2 * PL), F32),
-            pltpu.VMEM((HEL, NV, 6 * PL), BF16),
-            pltpu.VMEM((NS, HEL, 16, NB), BF16),
-            pltpu.VMEM((NS - 1, HEL, 16, NB), BF16),
+            pltpu.VMEM((16, 24, 2, 8, 128), F32),
+            pltpu.VMEM((2, 2, NV, 6 * PL), BF16),
+            pltpu.VMEM((2, 2, NS // 2, 2, 16, NB), F32),
+            pltpu.VMEM((2, 2, NS // 2, 16, NB), BF16),
+            pltpu.VMEM((2, 2, NS // 2, 16, NB), BF16),
+            pltpu.VMEM((NS // 2, HEL, 16, NB), BF16),
+            pltpu.VMEM((NS // 2 - 1, HEL, 16, NB), BF16),
             pltpu.VMEM((NS, 2 * NV, 128), BF16),
-            pltpu.VMEM((HEL, 16, NB), BF16),
-            pltpu.VMEM((2, 16, NV), BF16),
+            pltpu.VMEM((2, 2, 16, NB), BF16),
+            pltpu.VMEM((2, 2, 16, NB), BF16),
             dma((13,)), dma((6,)), dma((6,)), dma, dma, dma, dma, dma,
-            dma((20,)), dma((4,)), dma((16,)), dma, dma, dma, dma, dma, dma,
+            dma((20,)), dma((4,)), dma((16,)), dma, dma, dma((2,)), dma((2,)), dma, dma, dma, dma,
         ],
         compiler_params=pltpu.CompilerParams(collective_id=0, has_side_effects=True,
-                                             vmem_limit_bytes=60 * 1024 * 1024),
+                                             vmem_limit_bytes=48 * 1024 * 1024),
     )(momenta, jnp.transpose(coef_num, (2, 1, 0)), coef_den, lk, v, piece)
     return out.reshape(1, 2, 4, 4, 2, 8, NV)
 

time: 49.3 us -> 41.9 us (0.85); the launches traced: 49.1 us -> 41.1 us
  Pallas kernels: 42.7 us -> 34.7 us
    pallas_call x1, Pallas kernels: 42.7 us -> 34.7 us  [shards(): pl.pallas_call(kernel, out_shape=jax.ShapeDtypeStruct((2, 16, 2, 8, NV),...]
    unnamed x2 -> x10, local copies, waits for them, and re-layouts: 4.66 us -> 5.34 us
    dynamic_slice x2, local copies, waits for them, and re-layouts: 1.67 us -> 1.02 us  [shards(): piece = lax.dynamic_slice(per, (0, place, 0, core * 128), (NV, 1, 2, 128))]
where the time goes in v2:
time: 41.9 us; the launch traced here: 41.1 us
  Pallas kernels  34.7 us (83%)
  local copies, waits for them, and re-layouts  6.36 us (15%)
    pallas_call x1, Pallas kernels, shards(): pl.pallas_call(kernel, out_shape=jax.ShapeDtypeStruct((2, 16, 2, 8, NV),...  34.7 us
    unnamed x10, local copies, waits for them, and re-layouts  5.34 us
    dynamic_slice x2, local copies, waits for them, and re-layouts, shards(): piece = lax.dynamic_slice(per, (0, place, 0, core * 128), (NV, 1, 2, 128))  1.02 us

profile of v2, /device:TPU:1, one launch (start us, length us, event | category | flops | bytes accessed | tf_op | source)
XLA Modules:
  0.0 41.1 jit_solution(14647045364508055127)
XLA Ops:
  0.0 1.0 %constant_dynamic-slice_fusion = bf16[256,1,2,128]{3,2,1,0:T(2,128)(2,1)S(1)} fusion(bf16[256,16,2,256]{3,2,1,0:T(2,128)(2,1)} %bitcast.19, s32[]{:T(128)S(6)} %select_n.42, s32[]{:T(128)S(6)} %select_n.43), kind=kLoop, calls=%fused_computation.1 | loop fusion | bytes 262152 | tf_op jit(solution)/shard_map/dynamic_slice | solution.py:388
  1.0 1.6 %copy.10 = bf16[1,2,256,3,2,256]{5,2,1,4,3,0:T(8,128)(2,1)S(1)} copy(bf16[1,2,256,3,2,256]{5,4,3,2,1,0:T(2,128)(2,1)} %param.6) | data formatting | bytes 3145728 | tf_op args[0]
  2.7 0.0 copy-start
  2.7 0.9 %copy-done = f32[1,3,3,3,2,2,256]{6,5,4,3,2,1,0:T(2,128)S(1)} copy-done((f32[1,3,3,3,2,2,256]{6,5,4,3,2,1,0:T(2,128)S(1)}, f32[1,3,3,3,2,2,256]{6,5,4,3,2,1,0:T(2,128)}, u32[]{:S(2)}) %copy-start) | copy-done | bytes 110616
  3.6 0.0 copy-start.1
  3.6 0.7 %copy-done.1 = s32[4,2,3]{0,1,2:T(2,128)S(1)} copy-done((s32[4,2,3]{0,1,2:T(2,128)S(1)}, s32[4,2,3]{0,1,2:T(2,128)}, u32[]{:S(2)}) %copy-start.1) | copy-done | bytes 120
  4.3 0.0 copy-start.2
  4.3 0.7 %copy-done.2 = s32[2,3]{1,0:T(2,128)S(1)} copy-done((s32[2,3]{1,0:T(2,128)S(1)}, s32[2,3]{1,0:T(2,128)}, u32[]{:S(2)}) %copy-start.2) | copy-done | bytes 48
  4.9 0.0 copy-start.3
  4.9 0.7 %copy-done.3 = s32[4]{0:T(128)S(1)} copy-done((s32[4]{0:T(128)S(1)}, s32[4]{0:T(128)}, u32[]{:S(2)}) %copy-start.3) | copy-done | bytes 40
  5.6 34.7 %shard_map.64 = f32[2,16,2,8,256]{4,3,2,1,0:T(8,128)S(1)} custom-call(s32[2,3]{1,0:T(2,128)S(1)} %copy-done.2, s32[3,2,4]{2,1,0:T(2,128)S(1)} %bitcast.18, s32[4]{0:T(128)S(1)} %copy-done.3, f32[54,2,256]{2,1,0:T(2,128)S(1)} %bitcast.17, bf16[3,2,2,256,256]{4,3,2,1,0:T(8,128)(2,1)S(1)} %bitcast.14, bf16[512,128]{1,0:T(8,128)(2,1)S(1)} %bitcast.16), custom_call_target="tpu_custom_call" | custom-call | tf_op jit(solution)/shard_map/pallas_call | solution.py:393
  40.3 0.8 %copy.12 = f32[1,2,4,4,2,8,256]{6,5,4,3,2,1,0:T(8,128)} copy(f32[1,2,4,4,2,8,256]{6,5,4,3,2,1,0:T(8,128)S(1)} %bitcast.15) | data formatting | bytes 1048576
  (1 shorter events, 0.0 us)
Async XLA Ops:
  2.7 0.9 %copy-start = (f32[1,3,3,3,2,2,256]{6,5,4,3,2,1,0:T(2,128)S(1)}, f32[1,3,3,3,2,2,256]{6,5,4,3,2,1,0:T(2,128)}, u32[]{:S(2)}) copy-start(f32[1,3,3,3,2,2,256]{6,5,4,3,2,1,0:T(2,128)} %param.7) | copy-start | bytes 331780
  3.6 0.7 %copy-start.1 = (s32[4,2,3]{0,1,2:T(2,128)S(1)}, s32[4,2,3]{0,1,2:T(2,128)}, u32[]{:S(2)}) copy-start(s32[4,2,3]{0,1,2:T(2,128)} %param.9) | copy-start | bytes 292
  4.3 0.7 %copy-start.2 = (s32[2,3]{1,0:T(2,128)S(1)}, s32[2,3]{1,0:T(2,128)}, u32[]{:S(2)}) copy-start(s32[2,3]{1,0:T(2,128)} %mom.1) | copy-start | bytes 76
  4.9 0.7 %copy-start.3 = (s32[4]{0:T(128)S(1)}, s32[4]{0:T(128)}, u32[]{:S(2)}) copy-start(s32[4]{0:T(128)} %den.1) | copy-start | bytes 52

commit v3 on v2

--- a/solution.py
+++ b/solution.py
@@ -27,8 +27,8 @@
     return lax.dot_general(a, b, (((1,), (1,)), ((), ())), preferred_element_type=F32)
 
 
-def kernel(mom, num, den, lk, v, piece, out,
-           xp, xm, halo_l, wloc, wrem, bc, vs, perm, shf, part, dbuf, pf, pq, ps, pbuf, rbuf, tbuf, sbuf, obuf,
+def kernel(mom_h, num_h, den_h, lk_h, v, piece, out,
+           mom, num, den, lk, s_in, xp, xm, halo_l, wloc, wrem, bc, vs, perm, shf, part, dbuf, pf, pq, ps, pbuf, rbuf, tbuf, sbuf, obuf,
            s_halo, r_up, r_dn, r_lk, s_w, r_w, s_z, r_z, s_g, r_g1, r_g2, s_sib, r_sib, s_ps, r_ps, s_rs, r_rs, s_o, r_o):
     me = lax.axis_index("space")
     tm = lax.axis_index("tm")
@@ -70,6 +70,11 @@
     right1, left1 = move1(me, 1), move1(me, 3)
     right2, left2 = move2(me, 1), move2(me, 3)
 
+    fetches = [pltpu.make_async_copy(a, b, s_in.at[n])
+               for n, (a, b) in enumerate(((mom_h, mom), (num_h, num), (den_h, den), (lk_h, lk)))]
+    for cp in fetches:
+        cp.start()
+
     barrier = pltpu.get_barrier_semaphore()
 
     def same_core(d):
@@ -83,6 +88,8 @@
     for where in (plane_dev(cross), plane_dev(sib), dev(me, tm, 1 - op), dev(me, 1 - tm, 1 - op)):
         pl.semaphore_signal(barrier, inc=1, device_id=where, device_id_type=MESH)
 
+    for cp in fetches[:3]:
+        cp.wait()
     site = lax.broadcasted_iota(jnp.int32, (8, PL), 1)
     yy = site // LZ
     zz = site & (LZ - 1)
@@ -116,7 +123,7 @@
         up.start()
         dn.start()
         halo += [up, dn]
-    lk_copy = remote(lk.at[pl.ds(0, 18)], halo_l, s_halo.at[12], r_lk, plane_dev(nxt))
+    lk_copy = remote(lk_h.at[pl.ds(0, 18)], halo_l, s_halo.at[12], r_lk, plane_dev(nxt))
     lk_copy.start()
     halo.append(lk_copy)
     w_copy = remote(wloc, wrem, s_w, r_w, dev(me, tm, 1 - op))
@@ -144,6 +151,8 @@
     for q in range(4):
         for plane in range(2):
             shf[q, :, plane * PL:(plane + 1) * PL] = jnp.dot(vs[plane], perm[q], preferred_element_type=F32)
+
+    fetches[3].wait()
 
     @pl.loop(0, 18)
     def _(k):
@@ -387,15 +396,21 @@
     per = peram[0].reshape(NV, 16, 2, NV)
     piece = lax.dynamic_slice(per, (0, place, 0, core * 128), (NV, 1, 2, 128))
     piece = jnp.transpose(piece[:, 0], (1, 0, 2)).reshape(2 * NV, 128)
+    hb = lambda x: pltpu.with_memory_space_constraint(x, pltpu.MemorySpace.HBM)
     vm = pl.BlockSpec(memory_space=pltpu.VMEM)
-    sm = pl.BlockSpec(memory_space=pltpu.SMEM)
+    hbm = pl.BlockSpec(memory_space=pltpu.MemorySpace.HBM)
     dma = pltpu.SemaphoreType.DMA
     out = pl.pallas_call(
         kernel,
         out_shape=jax.ShapeDtypeStruct((2, 16, 2, 8, NV), F32),
-        in_specs=[sm, sm, sm, vm, vm, vm],
+        in_specs=[hbm, hbm, hbm, hbm, vm, vm],
         out_specs=vm,
         scratch_shapes=[
+            pltpu.SMEM((2, 3), jnp.int32),
+            pltpu.SMEM((3, 2, HEL), jnp.int32),
+            pltpu.SMEM((HEL,), jnp.int32),
+            pltpu.VMEM((54, 2, PL), F32),
+            dma((4,)),
             pltpu.VMEM((6, NB, 2 * PL), BF16),
             pltpu.VMEM((6, NB, 2 * PL), BF16),
             pltpu.VMEM((18, 2, PL), F32),
@@ -420,7 +435,7 @@
         ],
         compiler_params=pltpu.CompilerParams(collective_id=0, has_side_effects=True,
                                              vmem_limit_bytes=48 * 1024 * 1024),
-    )(momenta, jnp.transpose(coef_num, (2, 1, 0)), coef_den, lk, v, piece)
+    )(hb(momenta), hb(jnp.transpose(coef_num, (2, 1, 0))), hb(coef_den), hb(lk), v, piece)
     return out.reshape(1, 2, 4, 4, 2, 8, NV)
 
 

time: 41.9 us -> 38.4 us (0.916)
  local copies, waits for them, and re-layouts: 6.36 us -> 3.45 us
  Pallas kernels: 34.7 us -> 34.2 us
    unnamed x10 -> x2, local copies, waits for them, and re-layouts: 5.34 us -> 2.43 us
    pallas_call x1, Pallas kernels: 34.7 us -> 34.2 us  [shards(): pl.pallas_call(kernel, out_shape=jax.ShapeDtypeStruct((2, 16, 2, 8, NV),...]
where the time goes in v3:
time: 38.4 us; the launch traced here: 37.7 us
  Pallas kernels  34.2 us (89%)
  local copies, waits for them, and re-layouts  3.45 us (9%)
    pallas_call x1, Pallas kernels, shards(): pl.pallas_call(kernel, out_shape=jax.ShapeDtypeStruct((2, 16, 2, 8, NV),...  34.2 us
    unnamed x2, local copies, waits for them, and re-layouts  2.43 us
    dynamic_slice x2, local copies, waits for them, and re-layouts, shards(): piece = lax.dynamic_slice(per, (0, place, 0, core * 128), (NV, 1, 2, 128))  1.02 us

profile of v3, /device:TPU:1, one launch (start us, length us, event | category | flops | bytes accessed | tf_op | source)
XLA Modules:
  0.0 37.7 jit_solution(17133173633785228294)
XLA Ops:
  0.0 1.0 %constant_dynamic-slice_fusion = bf16[256,1,2,128]{3,2,1,0:T(2,128)(2,1)S(1)} fusion(bf16[256,16,2,256]{3,2,1,0:T(2,128)(2,1)} %bitcast.18, s32[]{:T(128)S(6)} %select_n.42, s32[]{:T(128)S(6)} %select_n.43), kind=kLoop, calls=%fused_computation.1 | loop fusion | bytes 262152 | tf_op jit(solution)/shard_map/dynamic_slice | solution.py:397
  1.0 1.6 %copy.10 = bf16[1,2,256,3,2,256]{5,2,1,4,3,0:T(8,128)(2,1)S(1)} copy(bf16[1,2,256,3,2,256]{5,4,3,2,1,0:T(2,128)(2,1)} %param.6) | data formatting | bytes 3145728 | tf_op args[0]
  2.7 34.2 %shard_map.64 = f32[2,16,2,8,256]{4,3,2,1,0:T(8,128)S(1)} custom-call(s32[2,3]{1,0:T(2,128)} %mom_h.1, s32[3,2,4]{2,1,0:T(2,128)} %bitcast.19, s32[4]{0:T(128)} %den_h.1, f32[54,2,256]{2,1,0:T(2,128)} %bitcast.17, bf16[3,2,2,256,256]{4,3,2,1,0:T(8,128)(2,1)S(1)} %bitcast.14, bf16[512,128]{1,0:T(8,128)(2,1)S(1)} %bitcast.16), custom_call_target="tpu_custom_call" | custom-call | tf_op jit(solution)/shard_map/pallas_call | solution.py:403
  36.9 0.8 %copy.12 = f32[1,2,4,4,2,8,256]{6,5,4,3,2,1,0:T(8,128)} copy(f32[1,2,4,4,2,8,256]{6,5,4,3,2,1,0:T(8,128)S(1)} %bitcast.15) | data formatting | bytes 1048576
  (1 shorter events, 0.0 us)

commit v4 on v3

--- a/solution.py
+++ b/solution.py
@@ -28,8 +28,8 @@
 
 
 def kernel(mom_h, num_h, den_h, lk_h, v, piece, out,
-           mom, num, den, lk, s_in, xp, xm, halo_l, wloc, wrem, bc, vs, perm, shf, part, dbuf, pf, pq, ps, pbuf, rbuf, tbuf, sbuf, obuf,
-           s_halo, r_up, r_dn, r_lk, s_w, r_w, s_z, r_z, s_g, r_g1, r_g2, s_sib, r_sib, s_ps, r_ps, s_rs, r_rs, s_o, r_o):
+           mom, num, den, lk, s_in, xp, xm, halo_l, wloc, wrem, bc, vs, perm, shf, part, dbuf, pf, pq, ps, pbuf, rbuf, tbuf, obuf,
+           s_halo, r_up, r_dn, r_lk, s_w, r_w, s_z, r_z, s_g, r_g1, r_g2, s_sib, r_sib, s_ps, r_ps, s_rs, r_rs):
     me = lax.axis_index("space")
     tm = lax.axis_index("tm")
     op = lax.axis_index("op")
@@ -84,8 +84,12 @@
     def _(d):
         pl.semaphore_signal(barrier, inc=1, device_id=plane_dev(same_core(d)), device_id_type=MESH)
 
+    @pl.loop(0, NS // 2)
+    def _(d):
+        pl.semaphore_signal(barrier, inc=1, device_id=dev(same_core(d), tm, 1 - op), device_id_type=MESH)
+
     cross = lax.rem(me + NS + 2 * core - 1, NS)
-    for where in (plane_dev(cross), plane_dev(sib), dev(me, tm, 1 - op), dev(me, 1 - tm, 1 - op)):
+    for where in (plane_dev(cross), plane_dev(sib), dev(me, 1 - tm, 1 - op)):
         pl.semaphore_signal(barrier, inc=1, device_id=where, device_id_type=MESH)
 
     for cp in fetches[:3]:
@@ -110,7 +114,7 @@
                     row = (h * 3 + j) * 2 + ri
                     wloc[plane, row:row + 1, :] = w[0:1]
 
-    pl.semaphore_wait(barrier, NS // 2 + 3)
+    pl.semaphore_wait(barrier, NS + 2)
 
     brow = pl.ds(pl.multiple_of(op * NB, NB), NB)
     halo = []
@@ -245,21 +249,26 @@
         g.start()
         return g
 
-    def to_sibling(k):
+    def to_sibling(k, n):
         ref = tbuf.at[k]
-        remote(ref, ref, s_sib, r_sib, plane_dev(sib)).start()
-
-    def spread(k, n):
+        remote(ref, ref, s_sib.at[n], r_sib.at[n], plane_dev(sib)).start()
+
+    def along(k, n):
         ahead.append((send(k, ALL, 4 + 2 * n, r_g2.at[2 * n], right2),
                       send(k, ALL, 5 + 2 * n, r_g2.at[2 * n + 1], left2)))
+
+    def over(k, n):
         ref = tbuf.at[k]
         g = remote(ref, ref, s_g.at[12 + n], r_g2.at[8 + n], dev(me, tm, 1 - op))
         g.start()
         across.append(g)
-        to_sibling(k)
-
-    EARLY = 16
-    run_tiles(0, EARLY // 2, (1, 2), False, False)
+        to_sibling(k, n)
+
+    def spread(k, n):
+        along(k, n)
+        over(k, n)
+
+    run_tiles(0, 16, (1, 2), False, False)
 
     z_copy.wait()
     ahead = []
@@ -267,7 +276,8 @@
     first = [send(came, ALL, 0, r_g1.at[0], right1), send(came, ALL, 1, r_g1.at[1], left1)]
     spread(came, 0)
 
-    run_tiles(EARLY // 2, EARLY, (1, 2), False, False)
+    run_tiles(16, 24, (1, 2), False, False)
+    run_tiles(24, 32, (1, 2), False, False)
 
     for cp in halo:
         cp.wait()
@@ -278,7 +288,16 @@
         for lt in range(2):
             bc[lt, 54 + k] = row[:, lt * 128:lt * 128 + 128]
 
-    run_tiles(0, EARLY, (0,), True, True)
+    run_tiles(0, 8, (0,), True, True)
+
+    for g in first:
+        g.wait()
+    kl, kr, ko = move1(came, 3), move1(came, 1), move1(came, 2)
+    onward = [send(kl, LOW, 2, r_g1.at[2], right1), send(kr, HIGH, 3, r_g1.at[3], left1)]
+    spread(kl, 1)
+    spread(kr, 2)
+
+    run_tiles(8, 16, (0,), True, True)
 
     def products(half):
         for hp in range(2):
@@ -298,30 +317,21 @@
     def combine(half, g):
         g.wait()
         for hp in range(2):
-            pbuf[:, 2 * half + hp] = (pf[half, hp, :, core] + ps[half, hp].astype(F32)).astype(BF16)
+            pbuf[hp, :, half] = (pf[half, hp, :, core] + ps[half, hp].astype(F32)).astype(BF16)
+
+        @pl.loop(0, NS // 2)
+        def _(d):
+            owner = lax.rem(chip + d, NS // 2)
+            remote(pbuf.at[1 - op, owner, half], rbuf.at[NS // 2 - 1 + d, half], s_rs, r_rs,
+                   dev(owner * 2 + core, tm, 1 - op)).start()
 
         @pl.loop(1, NS // 2)
         def _(d):
             owner = lax.rem(chip + d, NS // 2)
-            remote(pbuf.at[owner, pl.ds(2 * half, 2)], rbuf.at[d - 1, pl.ds(2 * half, 2)], s_rs, r_rs,
+            remote(pbuf.at[op, owner, half], rbuf.at[d - 1, half], s_rs, r_rs,
                    plane_dev(owner * 2 + core)).start()
 
     early = products(0)
-
-    for g in first:
-        g.wait()
-    kl, kr, ko = move1(came, 3), move1(came, 1), move1(came, 2)
-    onward = [send(kl, LOW, 2, r_g1.at[2], right1), send(kr, HIGH, 3, r_g1.at[3], left1)]
-    spread(kl, 1)
-    spread(kr, 2)
-
-    run_tiles(EARLY, 22)
-    combine(0, early)
-    run_tiles(22, 27)
-
-    for g in onward:
-        g.wait()
-    spread(ko, 3)
 
     def turned(k, d):
         at = lax.rem(p2 + 2 * op, 4)
@@ -332,33 +342,39 @@
             g.wait()
         across[n].wait()
         k = (came, kl, kr, ko)[n]
-        to_sibling(turned(k, 3))
-        to_sibling(turned(k, 1))
-        to_sibling(turned(k, 2))
-
-    run_tiles(27, 32)
+        to_sibling(turned(k, 3), n)
+        to_sibling(turned(k, 1), n)
+        to_sibling(turned(k, 2), n)
+
+    settle(0)
+    run_tiles(16, 20, (0,), True, True)
+    combine(0, early)
+    run_tiles(20, 24, (0,), True, True)
+
+    for g in onward:
+        g.wait()
+    spread(ko, 3)
+
+    run_tiles(24, 32, (0,), True, True)
     combine(1, products(1))
 
-    for n in range(4):
+    for n in range(1, 4):
         settle(n)
 
-    whole = remote(pbuf.at[pl.ds(0, NS // 2 - 1)], rbuf, s_rs, r_rs, plane_dev(sib))
-    whole.wait_recv()
+    whole = remote(rbuf, rbuf, s_rs, r_rs, plane_dev(sib))
+    whole.wait()
 
     def add(d, acc):
         return acc + rbuf[d].astype(F32)
 
-    own = pf[:, :, chip, core] + ps[:, :, chip].astype(F32)
-    total = lax.fori_loop(0, NS // 2 - 1, add, own.reshape(4, 16, NB))
-    sbuf[...] = total.reshape(2, 2, 16, NB).astype(BF16)
-    o_copy = remote(sbuf.at[:, 1 - op], obuf.at[op], s_o, r_o, dev(me, tm, 1 - op))
-    o_copy.start()
-    obuf[op] = sbuf[:, op]
-    whole.wait_send()
-    o_copy.wait()
-
-    half = tbuf.at[pl.ds(0, 16)]
-    remote(half, half, s_sib, r_sib, plane_dev(sib)).wait()
+    own = pf[:, op, chip, core] + ps[:, op, chip].astype(F32)
+    obuf[op] = lax.fori_loop(0, NS // 2 - 1, add, own).astype(BF16)
+    other = lax.fori_loop(NS // 2, NS - 1, add, rbuf[NS // 2 - 1].astype(F32))
+    obuf[1 - op] = other.astype(BF16)
+
+    for n in range(4):
+        some = tbuf.at[pl.ds(0, 4)]
+        remote(some, some, s_sib.at[n], r_sib.at[n], plane_dev(sib)).wait()
 
     lane = lax.broadcasted_iota(jnp.int32, (16, NB), 1)
     low = lane < NB // 2
@@ -420,18 +436,17 @@
             pltpu.VMEM((2, 6 * NB, PL), BF16),
             pltpu.VMEM((4, PL, PL), BF16),
             pltpu.VMEM((4, 6 * NB, 2 * PL), F32),
-            pltpu.VMEM((16, 24, 2, 8, 128), F32),
+            pltpu.VMEM((32, 24, 2, 8, 128), F32),
             pltpu.VMEM((2, 2, NV, 6 * PL), BF16),
             pltpu.VMEM((2, 2, NS // 2, 2, 16, NB), F32),
             pltpu.VMEM((2, 2, NS // 2, 16, NB), BF16),
             pltpu.VMEM((2, 2, NS // 2, 16, NB), BF16),
-            pltpu.VMEM((NS // 2, HEL, 16, NB), BF16),
-            pltpu.VMEM((NS // 2 - 1, HEL, 16, NB), BF16),
+            pltpu.VMEM((2, NS // 2, 2, 16, NB), BF16),
+            pltpu.VMEM((NS - 1, 2, 16, NB), BF16),
             pltpu.VMEM((NS, 2 * NV, 128), BF16),
             pltpu.VMEM((2, 2, 16, NB), BF16),
-            pltpu.VMEM((2, 2, 16, NB), BF16),
             dma((13,)), dma((6,)), dma((6,)), dma, dma, dma, dma, dma,
-            dma((20,)), dma((4,)), dma((16,)), dma, dma, dma((2,)), dma((2,)), dma, dma, dma, dma,
+            dma((20,)), dma((4,)), dma((16,)), dma((4,)), dma((4,)), dma((2,)), dma((2,)), dma, dma,
         ],
         compiler_params=pltpu.CompilerParams(collective_id=0, has_side_effects=True,
                                              vmem_limit_bytes=48 * 1024 * 1024),

time: 38.4 us -> 36.8 us (0.958); the launches traced: 37.7 us -> 36.6 us
  Pallas kernels: 34.2 us -> 33.1 us
    pallas_call x1, Pallas kernels: 34.2 us -> 33.1 us  [shards(): pl.pallas_call(kernel, out_shape=jax.ShapeDtypeStruct((2, 16, 2, 8, NV),...]
where the time goes in v4:
time: 36.8 us; the launch traced here: 36.6 us
  Pallas kernels  33.1 us (90%)
  local copies, waits for them, and re-layouts  3.45 us (9%)
    pallas_call x1, Pallas kernels, shards(): pl.pallas_call(kernel, out_shape=jax.ShapeDtypeStruct((2, 16, 2, 8, NV),...  33.1 us
    unnamed x2, local copies, waits for them, and re-layouts  2.43 us
    dynamic_slice x2, local copies, waits for them, and re-layouts, shards(): piece = lax.dynamic_slice(per, (0, place, 0, core * 128), (NV, 1, 2, 128))  1.02 us

profile of v4, /device:TPU:1, one launch (start us, length us, event | category | flops | bytes accessed | tf_op | source)
XLA Modules:
  0.0 36.6 jit_solution(815977386624971231)
XLA Ops:
  0.0 1.0 %constant_dynamic-slice_fusion = bf16[256,1,2,128]{3,2,1,0:T(2,128)(2,1)S(1)} fusion(bf16[256,16,2,256]{3,2,1,0:T(2,128)(2,1)} %bitcast.18, s32[]{:T(128)S(6)} %select_n.42, s32[]{:T(128)S(6)} %select_n.43), kind=kLoop, calls=%fused_computation.1 | loop fusion | bytes 262152 | tf_op jit(solution)/shard_map/dynamic_slice | solution.py:413
  1.0 1.6 %copy.10 = bf16[1,2,256,3,2,256]{5,2,1,4,3,0:T(8,128)(2,1)S(1)} copy(bf16[1,2,256,3,2,256]{5,4,3,2,1,0:T(2,128)(2,1)} %param.6) | data formatting | bytes 3145728 | tf_op args[0]
  2.7 33.1 %shard_map.64 = f32[2,16,2,8,256]{4,3,2,1,0:T(8,128)S(1)} custom-call(s32[2,3]{1,0:T(2,128)} %mom_h.1, s32[3,2,4]{2,1,0:T(2,128)} %bitcast.19, s32[4]{0:T(128)} %den_h.1, f32[54,2,256]{2,1,0:T(2,128)} %bitcast.17, bf16[3,2,2,256,256]{4,3,2,1,0:T(8,128)(2,1)S(1)} %bitcast.14, bf16[512,128]{1,0:T(8,128)(2,1)S(1)} %bitcast.16), custom_call_target="tpu_custom_call" | custom-call | tf_op jit(solution)/shard_map/pallas_call | solution.py:419
  35.8 0.8 %copy.12 = f32[1,2,4,4,2,8,256]{6,5,4,3,2,1,0:T(8,128)} copy(f32[1,2,4,4,2,8,256]{6,5,4,3,2,1,0:T(8,128)S(1)} %bitcast.15) | data formatting | bytes 1048576
  (1 shorter events, 0.0 us)

commit v5 on v4

--- a/solution.py
+++ b/solution.py
@@ -91,6 +91,27 @@
     cross = lax.rem(me + NS + 2 * core - 1, NS)
     for where in (plane_dev(cross), plane_dev(sib), dev(me, 1 - tm, 1 - op)):
         pl.semaphore_signal(barrier, inc=1, device_id=where, device_id_type=MESH)
+
+    pl.semaphore_wait(barrier, NS + 2)
+
+    z_copy = remote(piece, tbuf.at[held(me, 1 - op)], s_z, r_z, dev(me, 1 - tm, 1 - op))
+    came = held(me, op)
+    z_copy.start()
+
+    brow = pl.ds(pl.multiple_of(op * NB, NB), NB)
+    halo = []
+    for f in range(6):
+        ri, c = f // 3, f % 3
+        up = remote(v.at[c, 0, ri, brow], xp.at[f, :, pl.ds(PL, PL)],
+                    s_halo.at[f], r_up.at[f], plane_dev(prv))
+        dn = remote(v.at[c, 1, ri, brow], xm.at[f, :, pl.ds(0, PL)],
+                    s_halo.at[6 + f], r_dn.at[f], plane_dev(nxt))
+        up.start()
+        dn.start()
+        halo += [up, dn]
+    lk_copy = remote(lk_h.at[pl.ds(0, 18)], halo_l, s_halo.at[12], r_lk, plane_dev(nxt))
+    lk_copy.start()
+    halo.append(lk_copy)
 
     for cp in fetches[:3]:
         cp.wait()
@@ -113,29 +134,8 @@
                     w = (phase[0][ri] * n0 + phase[1][ri] * n1) * inv[h]
                     row = (h * 3 + j) * 2 + ri
                     wloc[plane, row:row + 1, :] = w[0:1]
-
-    pl.semaphore_wait(barrier, NS + 2)
-
-    brow = pl.ds(pl.multiple_of(op * NB, NB), NB)
-    halo = []
-    for f in range(6):
-        ri, c = f // 3, f % 3
-        up = remote(v.at[c, 0, ri, brow], xp.at[f, :, pl.ds(PL, PL)],
-                    s_halo.at[f], r_up.at[f], plane_dev(prv))
-        dn = remote(v.at[c, 1, ri, brow], xm.at[f, :, pl.ds(0, PL)],
-                    s_halo.at[6 + f], r_dn.at[f], plane_dev(nxt))
-        up.start()
-        dn.start()
-        halo += [up, dn]
-    lk_copy = remote(lk_h.at[pl.ds(0, 18)], halo_l, s_halo.at[12], r_lk, plane_dev(nxt))
-    lk_copy.start()
-    halo.append(lk_copy)
     w_copy = remote(wloc, wrem, s_w, r_w, dev(me, tm, 1 - op))
     w_copy.start()
-
-    z_copy = remote(piece, tbuf.at[held(me, 1 - op)], s_z, r_z, dev(me, 1 - tm, 1 - op))
-    came = held(me, op)
-    z_copy.start()
 
     for f in range(6):
         ri, c = f // 3, f % 3

time: 36.8 us -> 36.8 us (level)
  no operation moved by 1% of the time
where the time goes in v5:
time: 36.8 us; the launch traced here: 36.6 us
  Pallas kernels  33.2 us (90%)
  local copies, waits for them, and re-layouts  3.45 us (9%)
    pallas_call x1, Pallas kernels, shards(): pl.pallas_call(kernel, out_shape=jax.ShapeDtypeStruct((2, 16, 2, 8, NV),...  33.2 us
    unnamed x2, local copies, waits for them, and re-layouts  2.43 us
    dynamic_slice x2, local copies, waits for them, and re-layouts, shards(): piece = lax.dynamic_slice(per, (0, place, 0, core * 128), (NV, 1, 2, 128))  1.02 us

profile of v5, /device:TPU:1, one launch (start us, length us, event | category | flops | bytes accessed | tf_op | source)
XLA Modules:
  0.0 36.6 jit_solution(13799306639343152052)
XLA Ops:
  0.0 1.0 %constant_dynamic-slice_fusion = bf16[256,1,2,128]{3,2,1,0:T(2,128)(2,1)S(1)} fusion(bf16[256,16,2,256]{3,2,1,0:T(2,128)(2,1)} %bitcast.18, s32[]{:T(128)S(6)} %select_n.42, s32[]{:T(128)S(6)} %select_n.43), kind=kLoop, calls=%fused_computation.1 | loop fusion | bytes 262152 | tf_op jit(solution)/shard_map/dynamic_slice | solution.py:413
  1.0 1.6 %copy.10 = bf16[1,2,256,3,2,256]{5,2,1,4,3,0:T(8,128)(2,1)S(1)} copy(bf16[1,2,256,3,2,256]{5,4,3,2,1,0:T(2,128)(2,1)} %param.6) | data formatting | bytes 3145728 | tf_op args[0]
  2.7 33.2 %shard_map.64 = f32[2,16,2,8,256]{4,3,2,1,0:T(8,128)S(1)} custom-call(s32[2,3]{1,0:T(2,128)} %mom_h.1, s32[3,2,4]{2,1,0:T(2,128)} %bitcast.19, s32[4]{0:T(128)} %den_h.1, f32[54,2,256]{2,1,0:T(2,128)} %bitcast.17, bf16[3,2,2,256,256]{4,3,2,1,0:T(8,128)(2,1)S(1)} %bitcast.14, bf16[512,128]{1,0:T(8,128)(2,1)S(1)} %bitcast.16), custom_call_target="tpu_custom_call" | custom-call | tf_op jit(solution)/shard_map/pallas_call | solution.py:419
  35.8 0.8 %copy.12 = f32[1,2,4,4,2,8,256]{6,5,4,3,2,1,0:T(8,128)} copy(f32[1,2,4,4,2,8,256]{6,5,4,3,2,1,0:T(8,128)S(1)} %bitcast.15) | data formatting | bytes 1048576
  (1 shorter events, 0.0 us)
